TPU v7x, 128 devices: a whole 4x4x4 slice. The times are simulated.
128 devices in a mesh: dp: 8 (over z, core), ctx: 16 (over x, y).
Axes of the slice: x: 4, y: 4, z: 4, core: 2. Of those that a mesh axis runs over, the one named last changes fastest.
Arguments:
- tokens: bfloat16 [32768, 2048], P(('dp', 'ctx')), parts along dimension 0, may hold values from -80 to 80
- qkv_weight: bfloat16 [2048, 3072], P('ctx'), may hold values from -0.125 to 0.125
- out_weight: bfloat16 [1024, 2048], P('ctx'), may hold values from -0.1875 to 0.1875
- prior_state: float32 [64, 128, 128], P('dp'), parts along dimension 0, may hold values from -240 to 240
- expert_ids: int32 [32768, 4], P(('dp', 'ctx')), parts along dimension 0, may hold values from 0 to 15, all different within a row; in each aligned block of 256 rows (0 to 255, 256 to 511, ...) at most 96 rows name the same one
- gate_weights: float32 [32768, 4], P(('dp', 'ctx')), parts along dimension 0, may hold values from 0.1 to 1
- expert_in: bfloat16 [16, 2048, 2048], P('ctx'), may hold values from -0.125 to 0.125
- expert_out: bfloat16 [16, 1024, 2048], P('ctx'), may hold values from -0.1875 to 0.1875
Outputs:
- layer_out: bfloat16 [32768, 2048], P(('dp', 'ctx')), parts along dimension 0
There are 8 independent parts, one for each index of `dp`. A program takes and returns all parts, laid end to end along the dimension named above; an argument that names none is the same for every part. Nothing has to cross between parts.
Inputs may be any that keep to these rules, and one draw needn't show every extreme that they name: `expert_ids`: within the 256 rows of one device no expert is named more than 96 times, and in some device's rows some expert is named exactly 96 times.
All inputs are finite; a program needn't handle non-finite values.
Results may differ from a plain program's by a relative error of at most 0.006.
Values may be sent and summed in bfloat16 or wider, within the bound.
No kernel may reach another device: no remote copies, remote signals or barrier semaphores. Data moves between devices by JAX's collectives and lax.ppermute only.
A program may use at most 128 MiB of HBM per device.

v0:
```python
import jax
import jax.numpy as jnp
from jax import lax
from jax.sharding import PartitionSpec as P

HEADS = 8
HD = 128
FF = 1024
SIDE = 4
GROUP = 4
EPSILON = 1e-05


def rms_rows(matrix):
    return matrix * lax.rsqrt(jnp.mean(matrix * matrix, axis=-1, keepdims=True) + EPSILON)


def swap_with(x, mask):
    return lax.ppermute(x, "dp", [(i, i ^ mask) for i in range(lax.axis_size("dp"))])


def shift_ctx(x, dx, dy):
    pairs = [
        (a * SIDE + b, (a + dx) % SIDE * SIDE + (b + dy) % SIDE)
        for a in range(SIDE)
        for b in range(SIDE)
    ]
    return lax.ppermute(x, "ctx", pairs)


def gather_by_exchange(x, axis):
    count = lax.axis_size(axis)
    spread = jnp.broadcast_to(x[None], (count,) + x.shape)
    return lax.all_to_all(spread, axis, split_axis=0, concat_axis=0, tiled=True)


def routing(expert_ids, gate_weights, experts, capacity):
    rows = expert_ids.shape[0]
    names = jnp.arange(experts, dtype=jnp.int32)
    hit = expert_ids[:, :, None] == names
    member = jnp.any(hit, axis=1)
    gate = jnp.sum(jnp.where(hit, gate_weights[:, :, None], 0.0), axis=1)
    order = jnp.arange(rows, dtype=jnp.int32)
    earlier = (order[:, None] > order[None, :]).astype(jnp.bfloat16)
    slot = jnp.dot(earlier, member.astype(jnp.bfloat16), preferred_element_type=jnp.float32)
    slot = jnp.where(member, slot.astype(jnp.int32), -1)
    slots = jnp.arange(capacity, dtype=jnp.int32)
    taken_out = slot.T[:, None, :] == slots[None, :, None]
    taken_back = slot[:, :, None] == slots[None, None, :]
    send = taken_out.astype(jnp.bfloat16).reshape(experts * capacity, rows)
    high = gate.astype(jnp.bfloat16)
    low = (gate - high.astype(jnp.float32)).astype(jnp.bfloat16)
    zero = jnp.zeros((), jnp.bfloat16)
    weigh = lambda g: jnp.where(taken_back, g[:, :, None], zero).reshape(rows, experts * capacity)
    return (send, jnp.concatenate([weigh(high), weigh(low)], axis=0))


def shards(
    tokens, qkv_weight, out_weight, prior_state, expert_ids, gate_weights, expert_in, expert_out
):
    rows, width = tokens.shape
    width_heads = HEADS * HD
    experts = lax.axis_size("ctx")
    capacity = 3 * rows * expert_ids.shape[1] // (2 * experts)
    own_heads = HEADS // GROUP
    own_width = own_heads * HD
    place = lax.axis_index("dp") % GROUP
    column = lax.axis_index("ctx") // SIDE
    row = lax.axis_index("ctx") % SIDE
    part = lambda n: lax.dynamic_slice_in_dim(
        qkv_weight, n * width_heads + place * own_width, own_width, axis=1
    )
    own_weight = jnp.concatenate([part(0), part(1), part(2)], axis=1)
    out_full = lax.all_gather(out_weight, "ctx", axis=0, tiled=True)
    normed = rms_rows(tokens.astype(jnp.float32)).astype(jnp.bfloat16)
    far = swap_with(normed, 2)
    near = swap_with(normed, 1)
    prior = [lax.dynamic_slice_in_dim(prior_state, place * own_heads, own_heads, axis=0)]
    for other in range(1, GROUP):
        theirs = lax.dynamic_slice_in_dim(
            prior_state, (place ^ other) * own_heads, own_heads, axis=0
        )
        prior.append(swap_with(theirs, other))
    prior = jnp.stack(prior)
    weight = gather_by_exchange(own_weight, "ctx").reshape(width, 3 * own_width)
    diagonal = swap_with(far, 1)
    everyone = jnp.concatenate([normed, near, far, diagonal], axis=0)
    send, weigh = routing(expert_ids, gate_weights, experts, capacity)
    projected = jnp.dot(everyone, weight, preferred_element_type=jnp.float32)
    split = lambda m: m.astype(jnp.bfloat16).reshape(GROUP, rows, own_heads, HD)
    queries = split(jax.nn.silu(projected[:, :own_width]))
    key_rows = split(jax.nn.silu(projected[:, own_width : 2 * own_width]))
    value_rows = split(projected[:, 2 * own_width :])
    state = jnp.einsum("jthd,jthe->jhde", key_rows, value_rows, preferred_element_type=jnp.float32)
    sent = state.astype(jnp.bfloat16)
    in_row = [shift_ctx(sent, 0, d).astype(jnp.float32) for d in range(1, SIDE)]
    total = (state + in_row[0] + in_row[1] + in_row[2]).astype(jnp.bfloat16)
    across = [shift_ctx(total, d, 0).astype(jnp.float32) for d in range(1, SIDE)]
    carried = prior
    for d in range(1, SIDE):
        carried = carried + jnp.where(row >= d, in_row[d - 1], 0.0)
        carried = carried + jnp.where(column >= d, across[d - 1], 0.0)
    scores = jnp.einsum("jthd,jshd->jhts", queries, key_rows, preferred_element_type=jnp.float32)
    order = jnp.arange(rows, dtype=jnp.int32)
    scores = jnp.where(order[:, None] >= order[None, :], scores, 0.0).astype(jnp.bfloat16)
    inside = jnp.einsum("jhts,jshe->jthe", scores, value_rows, preferred_element_type=jnp.float32)
    high = carried.astype(jnp.bfloat16)
    low = (carried - high.astype(jnp.float32)).astype(jnp.bfloat16)
    from_state = jnp.einsum(
        "jthd,jhde->jthe", queries, high, preferred_element_type=jnp.float32
    ) + jnp.einsum("jthd,jhde->jthe", queries, low, preferred_element_type=jnp.float32)
    head_normed = rms_rows(from_state + inside).astype(jnp.bfloat16)
    head_normed = head_normed.reshape(GROUP, rows, own_width)
    back = [head_normed[0]] + [swap_with(head_normed[j], j) for j in range(1, GROUP)]
    back = jnp.stack(back)
    ordered = [lax.dynamic_index_in_dim(back, b ^ place, 0, keepdims=False) for b in range(GROUP)]
    attended = jnp.dot(
        jnp.concatenate(ordered, axis=1), out_full, preferred_element_type=jnp.float32
    )
    hidden = (tokens.astype(jnp.float32) + attended).astype(jnp.bfloat16)
    moe_in = rms_rows(hidden.astype(jnp.float32)).astype(jnp.bfloat16)
    outgoing = jnp.dot(send, moe_in, preferred_element_type=jnp.float32).astype(jnp.bfloat16)
    outgoing = outgoing.reshape(experts, capacity, width)
    arrived = lax.all_to_all(outgoing, "ctx", split_axis=0, concat_axis=0, tiled=True)
    grouped = arrived.reshape(experts * capacity, width)
    gate_up = jnp.dot(grouped, expert_in[0], preferred_element_type=jnp.float32)
    middle = (jax.nn.silu(gate_up[:, :FF]) * gate_up[:, FF:]).astype(jnp.bfloat16)
    result = jnp.dot(middle, expert_out[0], preferred_element_type=jnp.float32).astype(jnp.bfloat16)
    returned = lax.all_to_all(
        result.reshape(experts, capacity, width), "ctx", split_axis=0, concat_axis=0, tiled=True
    ).reshape(experts * capacity, width)
    combined = jnp.dot(weigh, returned, preferred_element_type=jnp.float32)
    return (hidden.astype(jnp.float32) + (combined[:rows] + combined[rows:])).astype(jnp.bfloat16)


def solution(mesh):
    return jax.shard_map(
        shards,
        mesh=mesh,
        in_specs=(
            P(("dp", "ctx"), None),
            P("ctx", None),
            P("ctx", None),
            P("dp", None, None),
            P(("dp", "ctx"), None),
            P(("dp", "ctx"), None),
            P("ctx", None, None),
            P("ctx", None, None),
        ),
        out_specs=P(("dp", "ctx"), None),
        check_vma=False,
    )
```

profile of v0, /device:TPU:124, one launch (start us, length us, event | category | flops | bytes accessed | tf_op | source)
XLA Modules:
  0.0 372.2 jit_solution(13127794874098399859)
XLA Ops:
  6.5 0.7 all-gather.2.cloned.1.call-update
  7.3 0.9 constant_dynamic-slice_fusion.2
  8.2 0.0 copy-start
  8.2 2.1 broadcast_in_dim.77
  10.3 7.1 %all-to-all-start = ((bf16[16,128,768]{2,1,0:T(8,128)(2,1)}), bf16[16,128,768]{2,1,0:T(8,128)(2,1)}, u32[]{:S(2)}, u32[]{:S(2)}) async-start(bf16[16,128,768]{2,1,0:T(8,128)(2,1)} %broadcast_in_dim.77), calls=%async_computation | async-start | bytes 6291456 | tf_op jit(solution)/shard_map/all_to_all | solution.py:34
  17.4 0.3 fusion.15
  17.7 0.2 fusion.16
  18.0 0.5 collective-permute-start.4
  18.5 23.9 %collective-permute-done.4 = bf16[256,2048]{1,0:T(8,128)(2,1)S(1)} collective-permute-done((bf16[256,2048]{1,0:T(8,128)(2,1)S(1)}, bf16[256,2048]{1,0:T(8,128)(2,1)S(1)}, u32[]{:S(2)}, u32[]{:S(2)}) %collective-permute-start.4) | collective-permute-done | bytes 1048608 | tf_op jit(solution)/shard_map/ppermute | solution.py:19
  42.4 0.0 collective-permute-done.3
  42.4 1.0 copy-done.6
  43.4 1.8 collective-permute-done.5
  45.2 18.2 %all-to-all-done = bf16[16,128,768]{2,1,0:T(8,128)(2,1)} async-done(((bf16[16,128,768]{2,1,0:T(8,128)(2,1)}), bf16[16,128,768]{2,1,0:T(8,128)(2,1)}, u32[]{:S(2)}, u32[]{:S(2)}) %all-to-all-start) | async-done | bytes 3145760 | tf_op jit(solution)/shard_map/all_to_all | solution.py:34
  63.4 5.9 %fusion.3 = f32[1024,768]{1,0:T(8,128)S(1)} fusion(bf16[2048,768]{1,0:T(8,128)(2,1)} %bitcast.4, bf16[256,2048]{1,0:T(8,128)(2,1)} %collective-permute-done.5, bf16[256,2048]{1,0:T(8,128)(2,1)S(1)} %collective-permute-done.4, bf16[256,2048]{1,0:T(8,128)(2,1)} %copy-done.6, bf16[256,2048]{1,0:T(8,128)(2,1)S(1)} %fusion.16), kind=kOutput, calls=%fused_computation.6 | convolution fusion | flops 3238002688 | bytes 10485760 | tf_op jit(solution)/shard_map/dot_general | solution.py:89
  69.4 0.1 slice.76
  69.4 1.4 multiply_convert_fusion.2
  70.8 0.1 reshape.81
  70.9 0.1 reshape.82
  71.1 0.4 copy.36
  71.4 0.0 copy-start.1
  71.5 1.1 fusion.66
  72.5 2.0 collective-permute-start.7
  74.5 0.1 collective-permute-start.8
  74.5 1.9 dynamic-slice_bitcast_fusion.4
  76.4 0.0 collective-permute-start
  76.4 11.1 %collective-permute-done.6 = bf16[4,2,128,128]{3,2,1,0:T(8,128)(2,1)S(1)} collective-permute-done((bf16[4,2,128,128]{3,2,1,0:T(8,128)(2,1)}, bf16[4,2,128,128]{3,2,1,0:T(8,128)(2,1)S(1)}, u32[]{:S(2)}, u32[]{:S(2)}) %collective-permute-start.6) | collective-permute-done | bytes 262176 | tf_op jit(solution)/shard_map/ppermute | solution.py:28
  87.5 1.6 collective-permute-done.7
  89.1 8.3 %collective-permute-done.8 = bf16[4,2,128,128]{3,2,1,0:T(8,128)(2,1)} collective-permute-done((bf16[4,2,128,128]{3,2,1,0:T(8,128)(2,1)}, bf16[4,2,128,128]{3,2,1,0:T(8,128)(2,1)}, u32[]{:S(2)}, u32[]{:S(2)}) %collective-permute-start.8) | collective-permute-done | bytes 262176 | tf_op jit(solution)/shard_map/ppermute | solution.py:28
  97.4 1.9 fusion.40
  99.2 0.8 collective-permute-start.10
  100.1 2.0 collective-permute-start.9
  102.1 0.6 collective-permute-start.1
  102.8 0.1 eq.63
  102.9 0.7 iota_compare_fusion.1
  103.5 0.1 reshape.83
  103.6 5.1 %collective-permute-done.1 = f32[2,128,128]{2,1,0:T(8,128)} collective-permute-done((f32[2,128,128]{2,1,0:T(8,128)}, f32[2,128,128]{2,1,0:T(8,128)}, u32[]{:S(2)}, u32[]{:S(2)}) %collective-permute-start.1) | collective-permute-done | bytes 131104 | tf_op jit(solution)/shard_map/ppermute | solution.py:19
  108.7 0.0 collective-permute-done.2
  108.8 0.7 collective-permute-done.10
  109.5 0.8 collective-permute-done.11
  110.3 1.9 collective-permute-done.9
  112.2 1.7 fusion.39
  113.9 0.3 fusion.54
  114.2 1.3 convolution_add_fusion
  115.6 2.9 multiply_reduce_fusion
  118.5 1.3 multiply_convert_fusion
  119.9 0.6 collective-permute-start.13
  120.4 1.7 collective-permute-start.12
  122.1 0.2 fusion.29
  122.3 0.3 bitcast_compare_fusion
  122.6 3.7 collective-permute-done.13
  126.2 0.1 pad_maximum_fusion
  126.4 0.0 all-gather.2.cloned.1.call-done
  126.4 3.6 fusion.17
  130.0 0.0 slice-start
  130.0 1.9 convolution_convert_fusion
  131.9 0.0 slice-start.1
  131.9 80.6 %all_to_all.15 = bf16[16,96,2048]{2,1,0:T(8,128)(2,1)S(1)} all-to-all(bf16[16,96,2048]{2,1,0:T(8,128)(2,1)S(1)} %bitcast.54), channel_id=1, replica_groups=mesh['dp'=8,'ctx'=16] {'ctx'}, dimensions={0} | all-to-all | bytes 12582912 | tf_op jit(solution)/shard_map/all_to_all | solution.py:124
  212.5 15.7 %fusion = f32[1536,2048]{1,0:T(8,128)} fusion(bf16[1536,2048]{1,0:T(8,128)(2,1)S(1)} %bitcast.56, bf16[1,2048,2048]{2,1,0:T(8,128)(2,1)S(1)} %bitcast.66), kind=kOutput, calls=%fused_computation | convolution fusion | flops 12884901888 | bytes 27262976 | tf_op jit(solution)/shard_map/dot_general | solution.py:126
  228.2 13.7 %convolution_convert_fusion.1 = bf16[1536,2048]{1,0:T(8,128)(2,1)} fusion(bf16[1,1024,2048]{2,1,0:T(8,128)(2,1)S(1)} %copy-done.5, f32[1536,2048]{1,0:T(8,128)} %fusion), kind=kOutput, calls=%fused_computation.3 | convolution fusion | flops 6455033856 | bytes 23068672 | tf_op jit(solution)/shard_map/dot_general | solution.py:128
  241.9 7.8 %all-to-all-start.2 = ((bf16[16,96,2048]{2,1,0:T(8,128)(2,1)}), bf16[16,96,2048]{2,1,0:T(8,128)(2,1)}, u32[]{:S(2)}, u32[]{:S(2)}) async-start(bf16[16,96,2048]{2,1,0:T(8,128)(2,1)} %bitcast.55), calls=%async_computation.2 | async-start | bytes 12582912 | tf_op jit(solution)/shard_map/all_to_all | solution.py:129
  249.7 0.3 fusion.25
  250.0 108.4 %all-to-all-done.2 = bf16[16,96,2048]{2,1,0:T(8,128)(2,1)} async-done(((bf16[16,96,2048]{2,1,0:T(8,128)(2,1)}), bf16[16,96,2048]{2,1,0:T(8,128)(2,1)}, u32[]{:S(2)}, u32[]{:S(2)}) %all-to-all-start.2) | async-done | bytes 6291488 | tf_op jit(solution)/shard_map/all_to_all | solution.py:129
  358.4 5.5 %fusion.20 = f32[512,2048]{1,0:T(8,128)S(1)} fusion(bf16[1536,2048]{1,0:T(8,128)(2,1)} %bitcast.27, bf16[256,1536]{0,1:T(8,128)(2,1)S(1)} %get-tuple-element.25, bf16[256,1536]{0,1:T(8,128)(2,1)S(1)} %get-tuple-element.24), kind=kOutput, calls=%fused_computation.30 | convolution fusion | flops 3224371200 | bytes 12058624 | tf_op jit(solution)/shard_map/dot_general | solution.py:132
  363.9 1.5 fusion.19
  (34 shorter events, 0.2 us)
Async XLA Ops:
  6.5 119.9 %all-gather.2.cloned.1.call-start = ((), (), s32[]{:S(2)}) async-start(), calls=%async_computation.3 | async-start | bytes 4456448 | tf_op jit(solution)/shard_map/all_gather | solution.py:74
  8.2 9.2 %copy-start = (bf16[256,2048]{1,0:T(8,128)(2,1)S(1)}, bf16[256,2048]{1,0:T(8,128)(2,1)}, u32[]{:S(2)}) copy-start(bf16[256,2048]{1,0:T(8,128)(2,1)} %param.8) | copy-start | bytes 3145732
  10.3 53.1 %all-to-all-start = ((bf16[16,128,768]{2,1,0:T(8,128)(2,1)}), bf16[16,128,768]{2,1,0:T(8,128)(2,1)}, u32[]{:S(2)}, u32[]{:S(2)}) async-start(bf16[16,128,768]{2,1,0:T(8,128)(2,1)} %broadcast_in_dim.77), calls=%async_computation | async-start | bytes 6291456 | tf_op jit(solution)/shard_map/all_to_all | solution.py:34
  18.0 24.4 %collective-permute-start.4 = (bf16[256,2048]{1,0:T(8,128)(2,1)S(1)}, bf16[256,2048]{1,0:T(8,128)(2,1)S(1)}, u32[]{:S(2)}, u32[]{:S(2)}) collective-permute-start(bf16[256,2048]{1,0:T(8,128)(2,1)S(1)} %fusion.16), channel_id=1, source_target_pairs={{0,32},{16,48},{32,0},{48,16},{64,96},{80,112},{96,64},{112,80},{1... | collective-permute-start | bytes 3145736 | tf_op jit(solution)/shard_map/ppermute | solution.py:19
  18.5 23.9 %collective-permute-start.3 = (bf16[256,2048]{1,0:T(8,128)(2,1)S(1)}, bf16[256,2048]{1,0:T(8,128)(2,1)S(1)}, u32[]{:S(2)}, u32[]{:S(2)}) collective-permute-start(bf16[256,2048]{1,0:T(8,128)(2,1)S(1)} %fusion.16), channel_id=1, source_target_pairs={{0,16},{16,0},{32,48},{48,32},{64,80},{80,64},{96,112},{112,96},{1... | collective-permute-start | bytes 3145736 | tf_op jit(solution)/shard_map/ppermute | solution.py:19
  42.4 2.8 collective-permute-start.5
  42.4 1.0 copy-start.6
  70.8 31.9 %copy-start.3 = (s32[256,4]{0,1:T(4,128)S(1)}, s32[256,4]{0,1:T(4,128)}, u32[]{:S(2)}) copy-start(s32[256,4]{0,1:T(4,128)} %param.12) | copy-start | bytes 12292
  71.4 32.1 %copy-start.1 = (bf16[1024,256]{1,0:T(8,128)(2,1)S(1)}, bf16[1024,256]{1,0:T(8,128)(2,1)}, u32[]{:S(2)}) copy-start(bf16[1024,256]{1,0:T(8,128)(2,1)} %get-tuple-element.8) | copy-start | bytes 1572868
  72.5 15.0 %collective-permute-start.6 = (bf16[4,2,128,128]{3,2,1,0:T(8,128)(2,1)}, bf16[4,2,128,128]{3,2,1,0:T(8,128)(2,1)S(1)}, u32[]{:S(2)}, u32[]{:S(2)}) collective-permute-start(bf16[4,2,128,128]{3,2,1,0:T(8,128)(2,1)} %get-tuple-element.26), channel_id=1, source_target_pairs={{0,1},{1,2},{2,3},{3,0},{4,5},{5,6},{6,7},{7,4},{8,9},{9,10},{10,1... | collective-permute-start | bytes 786440 | tf_op jit(solution)/shard_map/ppermute | solution.py:28
  72.5 16.6 %collective-permute-start.7 = (bf16[4,2,128,128]{3,2,1,0:T(8,128)(2,1)}, bf16[4,2,128,128]{3,2,1,0:T(8,128)(2,1)}, u32[]{:S(2)}, u32[]{:S(2)}) collective-permute-start(bf16[4,2,128,128]{3,2,1,0:T(8,128)(2,1)} %get-tuple-element.26), channel_id=1, source_target_pairs={{0,2},{1,3},{2,0},{3,1},{4,6},{5,7},{6,4},{7,5},{8,10},{9,11},{10,... | collective-permute-start | bytes 786440 | tf_op jit(solution)/shard_map/ppermute | solution.py:28
  74.5 22.9 %collective-permute-start.8 = (bf16[4,2,128,128]{3,2,1,0:T(8,128)(2,1)}, bf16[4,2,128,128]{3,2,1,0:T(8,128)(2,1)}, u32[]{:S(2)}, u32[]{:S(2)}) collective-permute-start(bf16[4,2,128,128]{3,2,1,0:T(8,128)(2,1)} %get-tuple-element.26), channel_id=1, source_target_pairs={{0,3},{1,0},{2,1},{3,2},{4,7},{5,4},{6,5},{7,6},{8,11},{9,8},{10,9... | collective-permute-start | bytes 786440 | tf_op jit(solution)/shard_map/ppermute | solution.py:28
  76.4 26.3 %collective-permute-start = (f32[2,128,128]{2,1,0:T(8,128)S(1)}, f32[2,128,128]{2,1,0:T(8,128)}, u32[]{:S(2)}, u32[]{:S(2)}) collective-permute-start(f32[2,128,128]{2,1,0:T(8,128)S(1)} %get-tuple-element.21), channel_id=1, source_target_pairs={{0,16},{16,0},{32,48},{48,32},{64,80},{80,64},{96,112},{112,96},{1... | collective-permute-start | bytes 393224 | tf_op jit(solution)/shard_map/ppermute | solution.py:19
  99.2 10.3 %collective-permute-start.10 = (bf16[4,2,128,128]{3,2,1,0:T(8,128)(2,1)}, bf16[4,2,128,128]{3,2,1,0:T(8,128)(2,1)}, u32[]{:S(2)}, u32[]{:S(2)}) collective-permute-start(bf16[4,2,128,128]{3,2,1,0:T(8,128)(2,1)} %fusion.40), channel_id=1, source_target_pairs={{0,8},{1,9},{2,10},{3,11},{4,12},{5,13},{6,14},{7,15},{8,0},{9,1},... | collective-permute-start | bytes 786440 | tf_op jit(solution)/shard_map/ppermute | solution.py:28
  100.1 10.2 %collective-permute-start.11 = (bf16[4,2,128,128]{3,2,1,0:T(8,128)(2,1)}, bf16[4,2,128,128]{3,2,1,0:T(8,128)(2,1)}, u32[]{:S(2)}, u32[]{:S(2)}) collective-permute-start(bf16[4,2,128,128]{3,2,1,0:T(8,128)(2,1)} %fusion.40), channel_id=1, source_target_pairs={{0,12},{1,13},{2,14},{3,15},{4,0},{5,1},{6,2},{7,3},{8,4},{9,5},{1... | collective-permute-start | bytes 786440 | tf_op jit(solution)/shard_map/ppermute | solution.py:28
  100.1 12.1 %collective-permute-start.9 = (bf16[4,2,128,128]{3,2,1,0:T(8,128)(2,1)}, bf16[4,2,128,128]{3,2,1,0:T(8,128)(2,1)}, u32[]{:S(2)}, u32[]{:S(2)}) collective-permute-start(bf16[4,2,128,128]{3,2,1,0:T(8,128)(2,1)} %fusion.40), channel_id=1, source_target_pairs={{0,4},{1,5},{2,6},{3,7},{4,8},{5,9},{6,10},{7,11},{8,12},{9,13},{1... | collective-permute-start | bytes 786440 | tf_op jit(solution)/shard_map/ppermute | solution.py:28
  102.1 6.7 %collective-permute-start.1 = (f32[2,128,128]{2,1,0:T(8,128)}, f32[2,128,128]{2,1,0:T(8,128)}, u32[]{:S(2)}, u32[]{:S(2)}) collective-permute-start(f32[2,128,128]{2,1,0:T(8,128)} %get-tuple-element.23), channel_id=1, source_target_pairs={{0,32},{16,48},{32,0},{48,16},{64,96},{80,112},{96,64},{112,80},{1... | collective-permute-start | bytes 393224 | tf_op jit(solution)/shard_map/ppermute | solution.py:19
  102.7 6.1 %collective-permute-start.2 = (f32[2,128,128]{2,1,0:T(8,128)}, f32[2,128,128]{2,1,0:T(8,128)}, u32[]{:S(2)}, u32[]{:S(2)}) collective-permute-start(f32[2,128,128]{2,1,0:T(8,128)} %get-tuple-element.22), channel_id=1, source_target_pairs={{0,48},{16,32},{32,16},{48,0},{64,112},{80,96},{96,80},{112,64},{1... | collective-permute-start | bytes 393224 | tf_op jit(solution)/shard_map/ppermute | solution.py:19
  113.9 1.7 copy-start.2
  119.9 6.4 %collective-permute-start.13 = (bf16[256,256]{0,1:T(8,128)(2,1)S(1)}, bf16[256,256]{0,1:T(8,128)(2,1)S(1)}, u32[]{:S(2)}, u32[]{:S(2)}) collective-permute-start(bf16[256,256]{0,1:T(8,128)(2,1)S(1)} %bitcast.62), channel_id=1, source_target_pairs={{0,32},{16,48},{32,0},{48,16},{64,96},{80,112},{96,64},{112,80},{1... | collective-permute-start | bytes 393224 | tf_op jit(solution)/shard_map/ppermute | solution.py:19
  120.4 5.8 %collective-permute-start.14 = (bf16[256,256]{0,1:T(8,128)(2,1)S(1)}, bf16[256,256]{0,1:T(8,128)(2,1)S(1)}, u32[]{:S(2)}, u32[]{:S(2)}) collective-permute-start(bf16[256,256]{0,1:T(8,128)(2,1)S(1)} %bitcast.60), channel_id=1, source_target_pairs={{0,48},{16,32},{32,16},{48,0},{64,112},{80,96},{96,80},{112,64},{1... | collective-permute-start | bytes 393224 | tf_op jit(solution)/shard_map/ppermute | solution.py:19
  120.4 5.8 %collective-permute-start.12 = (bf16[256,256]{0,1:T(8,128)(2,1)S(1)}, bf16[256,256]{0,1:T(8,128)(2,1)S(1)}, u32[]{:S(2)}, u32[]{:S(2)}) collective-permute-start(bf16[256,256]{0,1:T(8,128)(2,1)S(1)} %bitcast.58), channel_id=1, source_target_pairs={{0,16},{16,0},{32,48},{48,32},{64,80},{80,64},{96,112},{112,96},{1... | collective-permute-start | bytes 393224 | tf_op jit(solution)/shard_map/ppermute | solution.py:19
  130.0 82.5 %slice-start = ((s8[8388608]{0:T(1024)(128)(4,1)}), s8[4194304]{0:T(1024)(128)(4,1)S(1)}, s32[]{:S(2)}) async-start(s8[8388608]{0:T(1024)(128)(4,1)} %bitcast.65), calls=%async_computation.4 | async-start | bytes 8388608
  131.9 80.6 %slice-start.1 = ((s8[8388608]{0:T(1024)(128)(4,1)}), s8[4194304]{0:T(1024)(128)(4,1)S(1)}, s32[]{:S(2)}) async-start(s8[8388608]{0:T(1024)(128)(4,1)} %bitcast.65), calls=%async_computation.5 | async-start | bytes 8388608
  212.5 15.7 %copy-start.5 = (bf16[1,1024,2048]{2,1,0:T(8,128)(2,1)S(1)}, bf16[1,1024,2048]{2,1,0:T(8,128)(2,1)}, u32[]{:S(2)}) copy-start(bf16[1,1024,2048]{2,1,0:T(8,128)(2,1)} %param.15) | copy-start | bytes 12582916
  241.9 7.8 %copy-start.4 = (f32[256,4]{0,1:T(4,128)S(1)}, f32[256,4]{0,1:T(4,128)}, u32[]{:S(2)}) copy-start(f32[256,4]{0,1:T(4,128)} %param.13) | copy-start | bytes 12292
  241.9 116.5 %all-to-all-start.2 = ((bf16[16,96,2048]{2,1,0:T(8,128)(2,1)}), bf16[16,96,2048]{2,1,0:T(8,128)(2,1)}, u32[]{:S(2)}, u32[]{:S(2)}) async-start(bf16[16,96,2048]{2,1,0:T(8,128)(2,1)} %bitcast.55), calls=%async_computation.2 | async-start | bytes 12582912 | tf_op jit(solution)/shard_map/all_to_all | solution.py:129
Sparse Core Ops, SparseCore 0:
  9.5 89.8 all-gather.1
where the time goes:
time: 373 us; the launch traced here: 372 us
  waiting for transfers between devices  186 us (50%)
  blocking collectives  80.6 us (22%)
  matrix products  52.1 us (14%)
  starting transfers between devices  23.1 us (6%)
  between operations  13.7 us (4%)
  other arithmetic  9.66 us (3%)
  local copies, waits for them, and re-layouts  6.84 us (2%)
    all_to_all x1, waiting for transfers between devices, shards(): lax.all_to_all(result.reshape(experts, capacity, width), 'ctx', split_axi...  108 us
    all_to_all x1, blocking collectives, shards(): lax.all_to_all(outgoing, 'ctx', split_axis=0, concat_axis=0, tiled=True)  80.6 us
    ppermute x9, waiting for transfers between devices, swap_with(): lax.ppermute(x, 'dp', [(i, i ^ mask) for i in range(lax.axis_size('dp'))])  34.6 us
    ppermute x6, waiting for transfers between devices, shift_ctx(): return lax.ppermute(x, 'ctx', pairs)  24.3 us
    all_to_all x1, waiting for transfers between devices, gather_by_exchange(): return lax.all_to_all(spread, axis, split_axis=0, concat_axis=0, tiled=True)  18.2 us
    dot_general x1, matrix products, shards(): gate_up = jnp.dot(grouped, expert_in[0], preferred_element_type=jnp.float32)  15.7 us
    dot_general x1, matrix products, shards(): jnp.dot(middle, expert_out[0], preferred_element_type=jnp.float32)  13.7 us
    all_to_all x1, starting transfers between devices, shards(): lax.all_to_all(result.reshape(experts, capacity, width), 'ctx', split_axi...  7.81 us
  transfers between devices with their start and end apart: 18, of which 12 were waited for; matrix products, arithmetic and copies ran while one was open for 7% of the time, Pallas kernels for 0%

commit v1 on v0

--- a/solution.py
+++ b/solution.py
@@ -9,6 +9,23 @@
 SIDE = 4
 GROUP = 4
 EPSILON = 1e-05
+
+
+def spread_the_pages(field, array_axis, v0):
+    a_next = field.shape
+    return jnp.moveaxis(
+        field.reshape(
+            *a_next[:array_axis], v0, a_next[array_axis] // v0, *a_next[array_axis + 1 :]
+        ),
+        array_axis,
+        0,
+    )
+
+
+def _arrange_levels_all(local, out_dim):
+    local = jnp.moveaxis(local, 0, out_dim)
+    w2 = local.shape
+    return local.reshape(*w2[:out_dim], w2[out_dim] * w2[out_dim + 1], *w2[out_dim + 2 :])
 
 
 def rms_rows(matrix):
@@ -121,7 +138,15 @@
     moe_in = rms_rows(hidden.astype(jnp.float32)).astype(jnp.bfloat16)
     outgoing = jnp.dot(send, moe_in, preferred_element_type=jnp.float32).astype(jnp.bfloat16)
     outgoing = outgoing.reshape(experts, capacity, width)
-    arrived = lax.all_to_all(outgoing, "ctx", split_axis=0, concat_axis=0, tiled=True)
+    block_next, shaped = (lax.axis_size("ctx"), lax.axis_index("ctx"))
+    val = spread_the_pages(outgoing, 0, block_next)
+    pool = [val[shaped]]
+    for hop_no in range(1, block_next):
+        v_next = val[shaped ^ hop_no]
+        pool.append(lax.ppermute(v_next, "ctx", [(w, w ^ hop_no) for w in range(block_next)]))
+    passed = jnp.stack(pool, 0)
+    val = passed[shaped ^ jnp.arange(block_next)]
+    arrived = _arrange_levels_all(val, 0)
     grouped = arrived.reshape(experts * capacity, width)
     gate_up = jnp.dot(grouped, expert_in[0], preferred_element_type=jnp.float32)
     middle = (jax.nn.silu(gate_up[:, :FF]) * gate_up[:, FF:]).astype(jnp.bfloat16)

time: 373 us -> 421 us (1.13)
  blocking collectives: 80.6 us -> 0 us
  waiting for transfers between devices: 186 us -> 264 us
  starting transfers between devices: 23.1 us -> 55.1 us
  local copies, waits for them, and re-layouts: 6.84 us -> 26.8 us
    all_to_all x1 -> x0, blocking collectives: 80.6 us -> none  [shards(): lax.all_to_all(outgoing, 'ctx', split_axis=0, concat_axis=0, tiled=True)]
    ppermute x0 -> x15, waiting for transfers between devices: none -> 77.4 us  [shards(): lax.ppermute(v_next, 'ctx', [(w, w ^ hop_no) for w in range(block_next)])]
    ppermute x0 -> x15, starting transfers between devices: none -> 32.7 us  [shards(): lax.ppermute(v_next, 'ctx', [(w, w ^ hop_no) for w in range(block_next)])]
    unnamed x18 -> x24, local copies, waits for them, and re-layouts: 1.01 us -> 12 us
    gather x0 -> x1, local copies, waits for them, and re-layouts: none -> 6.35 us  [shards(): val = passed[shaped ^ jnp.arange(block_next)]]
    dot_general x1, matrix products: 13.7 us -> 8.66 us  [shards(): jnp.dot(middle, expert_out[0], preferred_element_type=jnp.float32)]
  transfers between devices with their start and end apart: 18 -> 33, of which waited for: 12 -> 22; matrix products, arithmetic and copies ran while one was open for 7% -> 9% of each run, Pallas kernels for 0% -> 0%
where the time goes in v1:
time: 421 us; the launch traced here: 418 us
  waiting for transfers between devices  264 us (63%)
  starting transfers between devices  55.1 us (13%)
  matrix products  49.1 us (12%)
  local copies, waits for them, and re-layouts  26.8 us (6%)
  between operations  13.9 us (3%)
  other arithmetic  8.86 us (2%)
    all_to_all x1, waiting for transfers between devices, shards(): lax.all_to_all(result.reshape(experts, capacity, width), 'ctx', split_axi...  109 us
    ppermute x15, waiting for transfers between devices, shards(): lax.ppermute(v_next, 'ctx', [(w, w ^ hop_no) for w in range(block_next)])  77.4 us
    ppermute x9, waiting for transfers between devices, swap_with(): lax.ppermute(x, 'dp', [(i, i ^ mask) for i in range(lax.axis_size('dp'))])  34.5 us
    ppermute x15, starting transfers between devices, shards(): lax.ppermute(v_next, 'ctx', [(w, w ^ hop_no) for w in range(block_next)])  32.7 us
    ppermute x6, waiting for transfers between devices, shift_ctx(): return lax.ppermute(x, 'ctx', pairs)  24.3 us
    all_to_all x1, waiting for transfers between devices, gather_by_exchange(): return lax.all_to_all(spread, axis, split_axis=0, concat_axis=0, tiled=True)  18.2 us
    dot_general x1, matrix products, shards(): gate_up = jnp.dot(grouped, expert_in[0], preferred_element_type=jnp.float32)  17.6 us
    unnamed x24, local copies, waits for them, and re-layouts  12 us
  transfers between devices with their start and end apart: 33, of which 22 were waited for; matrix products, arithmetic and copies ran while one was open for 9% of the time, Pallas kernels for 0%

profile of v1, /device:TPU:124, one launch (start us, length us, event | category | flops | bytes accessed | tf_op | source)
XLA Modules:
  0.0 417.7 jit_solution(535788925579273158)
XLA Ops:
  7.3 0.9 constant_dynamic-slice_fusion.2
  8.2 2.1 broadcast_in_dim.78
  10.3 7.1 %all-to-all-start = ((bf16[16,128,768]{2,1,0:T(8,128)(2,1)}), bf16[16,128,768]{2,1,0:T(8,128)(2,1)}, u32[]{:S(2)}, u32[]{:S(2)}) async-start(bf16[16,128,768]{2,1,0:T(8,128)(2,1)} %broadcast_in_dim.78), calls=%async_computation | async-start | bytes 6291456 | tf_op jit(solution)/shard_map/all_to_all | solution.py:51
  18.5 23.9 %collective-permute-done.4 = bf16[256,2048]{1,0:T(8,128)(2,1)S(1)} collective-permute-done((bf16[256,2048]{1,0:T(8,128)(2,1)S(1)}, bf16[256,2048]{1,0:T(8,128)(2,1)S(1)}, u32[]{:S(2)}, u32[]{:S(2)}) %collective-permute-start.4) | collective-permute-done | bytes 1048608 | tf_op jit(solution)/shard_map/ppermute | solution.py:36
  42.4 1.0 copy-done.4
  43.4 1.8 collective-permute-done.5
  45.2 18.2 %all-to-all-done = bf16[16,128,768]{2,1,0:T(8,128)(2,1)} async-done(((bf16[16,128,768]{2,1,0:T(8,128)(2,1)}), bf16[16,128,768]{2,1,0:T(8,128)(2,1)}, u32[]{:S(2)}, u32[]{:S(2)}) %all-to-all-start) | async-done | bytes 3145760 | tf_op jit(solution)/shard_map/all_to_all | solution.py:51
  63.4 5.9 %fusion.3 = f32[1024,768]{1,0:T(8,128)S(1)} fusion(bf16[2048,768]{1,0:T(8,128)(2,1)} %bitcast.4, bf16[256,2048]{1,0:T(8,128)(2,1)} %collective-permute-done.5, bf16[256,2048]{1,0:T(8,128)(2,1)S(1)} %collective-permute-done.4, bf16[256,2048]{1,0:T(8,128)(2,1)} %copy-done.4, bf16[256,2048]{1,0:T(8,128)(2,1)S(1)} %fusion.16), kind=kOutput, calls=%fused_computation.7 | convolution fusion | flops 3238002688 | bytes 10485760 | tf_op jit(solution)/shard_map/dot_general | solution.py:106
  70.7 1.1 fusion.67
  71.7 2.0 collective-permute-start.7
  73.8 1.8 dynamic-slice_bitcast_fusion.19
  75.6 11.1 %collective-permute-done.6 = bf16[4,2,128,128]{3,2,1,0:T(8,128)(2,1)S(1)} collective-permute-done((bf16[4,2,128,128]{3,2,1,0:T(8,128)(2,1)}, bf16[4,2,128,128]{3,2,1,0:T(8,128)(2,1)S(1)}, u32[]{:S(2)}, u32[]{:S(2)}) %collective-permute-start.6) | collective-permute-done | bytes 262176 | tf_op jit(solution)/shard_map/ppermute | solution.py:45
  86.7 1.6 collective-permute-done.7
  88.3 8.3 %collective-permute-done.8 = bf16[4,2,128,128]{3,2,1,0:T(8,128)(2,1)} collective-permute-done((bf16[4,2,128,128]{3,2,1,0:T(8,128)(2,1)}, bf16[4,2,128,128]{3,2,1,0:T(8,128)(2,1)}, u32[]{:S(2)}, u32[]{:S(2)}) %collective-permute-start.8) | collective-permute-done | bytes 262176 | tf_op jit(solution)/shard_map/ppermute | solution.py:45
  96.6 1.9 fusion.40
  98.4 1.0 collective-permute-start.10
  99.4 2.0 collective-permute-start.9
  102.9 5.1 %collective-permute-done.1 = f32[2,128,128]{2,1,0:T(8,128)} collective-permute-done((f32[2,128,128]{2,1,0:T(8,128)}, f32[2,128,128]{2,1,0:T(8,128)}, u32[]{:S(2)}, u32[]{:S(2)}) %collective-permute-start.1) | collective-permute-done | bytes 131104 | tf_op jit(solution)/shard_map/ppermute | solution.py:36
  109.2 2.1 collective-permute-done.9
  111.4 1.7 fusion.39
  113.4 1.3 convolution_add_fusion
  114.7 3.0 multiply_reduce_fusion
  117.7 1.3 multiply_convert_fusion
  119.7 1.6 collective-permute-start.12
  121.9 3.6 collective-permute-done.13
  125.7 3.6 fusion.17
  129.3 1.9 convolution_convert_fusion
  131.2 1.9 dynamic-slice_bitcast_fusion
  133.1 2.4 collective-permute-start.15
  135.5 2.5 collective-permute-start.16
  138.3 1.2 collective-permute-start.18
  139.5 1.1 collective-permute-start.19
  140.6 4.4 %collective-permute-done.15 = bf16[1,96,2048]{2,1,0:T(8,128)(2,1)S(1)} collective-permute-done((bf16[1,96,2048]{2,1,0:T(8,128)(2,1)S(1)}, bf16[1,96,2048]{2,1,0:T(8,128)(2,1)S(1)}, u32[]{:S(2)}, u32[]{:S(2)}) %collective-permute-start.15) | collective-permute-done | bytes 393248 | tf_op jit(solution)/shard_map/ppermute | solution.py:146
  145.0 3.2 collective-permute-start.20
  149.0 24.0 %collective-permute-done.16 = bf16[1,96,2048]{2,1,0:T(8,128)(2,1)S(1)} collective-permute-done((bf16[1,96,2048]{2,1,0:T(8,128)(2,1)S(1)}, bf16[1,96,2048]{2,1,0:T(8,128)(2,1)S(1)}, u32[]{:S(2)}, u32[]{:S(2)}) %collective-permute-start.16) | collective-permute-done | bytes 393248 | tf_op jit(solution)/shard_map/ppermute | solution.py:146
  173.6 0.8 bitcast_dynamic-update-slice_fusion.13
  174.4 1.0 collective-permute-start.22
  176.1 2.5 collective-permute-start.23
  179.4 4.5 %collective-permute-start.24 = (bf16[1,96,2048]{2,1,0:T(8,128)(2,1)S(1)}, bf16[1,96,2048]{2,1,0:T(8,128)(2,1)S(1)}, u32[]{:S(2)}, u32[]{:S(2)}) collective-permute-start(bf16[1,96,2048]{2,1,0:T(8,128)(2,1)S(1)} %get-tuple-element.12), channel_id=1, source_target_pairs={{0,10},{1,11},{2,8},{3,9},{4,14},{5,15},{6,12},{7,13},{8,2},{9,3},... | collective-permute-start | bytes 1179656 | tf_op jit(solution)/shard_map/ppermute | solution.py:146
  184.7 2.1 collective-permute-start.25
  186.8 0.8 bitcast_dynamic-update-slice_fusion.9
  187.6 1.4 collective-permute-start.26
  189.7 3.3 collective-permute-done.22
  193.0 1.9 collective-permute-start.27
  194.9 0.8 bitcast_dynamic-update-slice_fusion.7
  195.7 6.2 %collective-permute-done.23 = bf16[1,96,2048]{2,1,0:T(8,128)(2,1)S(1)} collective-permute-done((bf16[1,96,2048]{2,1,0:T(8,128)(2,1)S(1)}, bf16[1,96,2048]{2,1,0:T(8,128)(2,1)S(1)}, u32[]{:S(2)}, u32[]{:S(2)}) %collective-permute-start.23) | collective-permute-done | bytes 393248 | tf_op jit(solution)/shard_map/ppermute | solution.py:146
  201.9 4.4 %collective-permute-start.28 = (bf16[1,96,2048]{2,1,0:T(8,128)(2,1)S(1)}, bf16[1,96,2048]{2,1,0:T(8,128)(2,1)S(1)}, u32[]{:S(2)}, u32[]{:S(2)}) collective-permute-start(bf16[1,96,2048]{2,1,0:T(8,128)(2,1)S(1)} %get-tuple-element.8), channel_id=1, source_target_pairs={{0,14},{1,15},{2,12},{3,13},{4,10},{5,11},{6,8},{7,9},{8,6},{9,7},... | collective-permute-start | bytes 1179656 | tf_op jit(solution)/shard_map/ppermute | solution.py:146
  207.1 3.3 collective-permute-done.24
  210.5 3.7 collective-permute-start.29
  214.9 5.4 %collective-permute-done.25 = bf16[1,96,2048]{2,1,0:T(8,128)(2,1)S(1)} collective-permute-done((bf16[1,96,2048]{2,1,0:T(8,128)(2,1)S(1)}, bf16[1,96,2048]{2,1,0:T(8,128)(2,1)S(1)}, u32[]{:S(2)}, u32[]{:S(2)}) %collective-permute-start.25) | collective-permute-done | bytes 393248 | tf_op jit(solution)/shard_map/ppermute | solution.py:146
  221.0 5.0 %collective-permute-done.26 = bf16[1,96,2048]{2,1,0:T(8,128)(2,1)S(1)} collective-permute-done((bf16[1,96,2048]{2,1,0:T(8,128)(2,1)S(1)}, bf16[1,96,2048]{2,1,0:T(8,128)(2,1)S(1)}, u32[]{:S(2)}, u32[]{:S(2)}) %collective-permute-start.26) | collective-permute-done | bytes 393248 | tf_op jit(solution)/shard_map/ppermute | solution.py:146
  226.1 0.8 bitcast_dynamic-update-slice_fusion.3
  226.8 7.9 %collective-permute-done.27 = bf16[1,96,2048]{2,1,0:T(8,128)(2,1)S(1)} collective-permute-done((bf16[1,96,2048]{2,1,0:T(8,128)(2,1)S(1)}, bf16[1,96,2048]{2,1,0:T(8,128)(2,1)S(1)}, u32[]{:S(2)}, u32[]{:S(2)}) %collective-permute-start.27) | collective-permute-done | bytes 393248 | tf_op jit(solution)/shard_map/ppermute | solution.py:146
  235.5 8.0 %collective-permute-done.28 = bf16[1,96,2048]{2,1,0:T(8,128)(2,1)S(1)} collective-permute-done((bf16[1,96,2048]{2,1,0:T(8,128)(2,1)S(1)}, bf16[1,96,2048]{2,1,0:T(8,128)(2,1)S(1)}, u32[]{:S(2)}, u32[]{:S(2)}) %collective-permute-start.28) | collective-permute-done | bytes 393248 | tf_op jit(solution)/shard_map/ppermute | solution.py:146
  243.5 0.8 bitcast_dynamic-update-slice_fusion.1
  244.3 9.9 %collective-permute-done.29 = bf16[1,96,2048]{2,1,0:T(8,128)(2,1)S(1)} collective-permute-done((bf16[1,96,2048]{2,1,0:T(8,128)(2,1)S(1)}, bf16[1,96,2048]{2,1,0:T(8,128)(2,1)S(1)}, u32[]{:S(2)}, u32[]{:S(2)}) %collective-permute-start.29) | collective-permute-done | bytes 393248 | tf_op jit(solution)/shard_map/ppermute | solution.py:146
  254.3 0.8 bitcast_dynamic-update-slice_fusion
  255.1 6.4 %gather_fusion = bf16[16,96,2048]{2,1,0:T(8,128)(2,1)} fusion(bf16[16,96,2048]{2,1,0:T(8,128)(2,1)} %bitcast.53, s32[1024]{0:T(1024)S(1)} %pad_clamp_fusion), kind=kCustom, calls=%fused_computation | custom fusion | bytes 12582976 | tf_op jit(solution)/shard_map/gather | solution.py:148
  261.4 17.6 %fusion = f32[1536,2048]{1,0:T(8,128)S(1)} fusion(bf16[1536,2048]{1,0:T(8,128)(2,1)} %bitcast.119, bf16[1,2048,2048]{2,1,0:T(8,128)(2,1)} %param.14), kind=kOutput, calls=%fused_computation.1 | convolution fusion | flops 12884901888 | bytes 27262976 | tf_op jit(solution)/shard_map/dot_general | solution.py:151
  279.1 8.7 %convolution_convert_fusion.1 = bf16[1536,2048]{1,0:T(8,128)(2,1)} fusion(bf16[1,1024,2048]{2,1,0:T(8,128)(2,1)S(1)} %copy-done.3, f32[1536,2048]{1,0:T(8,128)S(1)} %fusion), kind=kOutput, calls=%fused_computation.4 | convolution fusion | flops 6455033856 | bytes 23068672 | tf_op jit(solution)/shard_map/dot_general | solution.py:153
  287.7 7.1 %all-to-all-start.1 = ((bf16[16,96,2048]{2,1,0:T(8,128)(2,1)}), bf16[16,96,2048]{2,1,0:T(8,128)(2,1)}, u32[]{:S(2)}, u32[]{:S(2)}) async-start(bf16[16,96,2048]{2,1,0:T(8,128)(2,1)} %bitcast.118), calls=%async_computation.1 | async-start | bytes 12582912 | tf_op jit(solution)/shard_map/all_to_all | solution.py:154
  295.1 108.7 %all-to-all-done.1 = bf16[16,96,2048]{2,1,0:T(8,128)(2,1)} async-done(((bf16[16,96,2048]{2,1,0:T(8,128)(2,1)}), bf16[16,96,2048]{2,1,0:T(8,128)(2,1)}, u32[]{:S(2)}, u32[]{:S(2)}) %all-to-all-start.1) | async-done | bytes 6291488 | tf_op jit(solution)/shard_map/all_to_all | solution.py:154
  403.9 5.5 %fusion.20 = f32[512,2048]{1,0:T(8,128)S(1)} fusion(bf16[1536,2048]{1,0:T(8,128)(2,1)} %bitcast.59, bf16[256,1536]{0,1:T(8,128)(2,1)S(1)} %get-tuple-element.41, bf16[256,1536]{0,1:T(8,128)(2,1)S(1)} %get-tuple-element.40), kind=kOutput, calls=%fused_computation.31 | convolution fusion | flops 3224371200 | bytes 12058624 | tf_op jit(solution)/shard_map/dot_general | solution.py:157
  409.4 1.5 fusion.19
  (73 shorter events, 15.5 us)
Async XLA Ops:
  6.5 10.9 %copy-start = (bf16[256,2048]{1,0:T(8,128)(2,1)S(1)}, bf16[256,2048]{1,0:T(8,128)(2,1)}, u32[]{:S(2)}) copy-start(bf16[256,2048]{1,0:T(8,128)(2,1)} %param.8) | copy-start | bytes 3145732
  6.5 119.1 %all-gather.2.cloned.1.call-start = ((), (), s32[]{:S(2)}) async-start(), calls=%async_computation.2 | async-start | bytes 4456448 | tf_op jit(solution)/shard_map/all_gather | solution.py:91
  10.3 53.1 %all-to-all-start = ((bf16[16,128,768]{2,1,0:T(8,128)(2,1)}), bf16[16,128,768]{2,1,0:T(8,128)(2,1)}, u32[]{:S(2)}, u32[]{:S(2)}) async-start(bf16[16,128,768]{2,1,0:T(8,128)(2,1)} %broadcast_in_dim.78), calls=%async_computation | async-start | bytes 6291456 | tf_op jit(solution)/shard_map/all_to_all | solution.py:51
  18.0 24.4 %collective-permute-start.4 = (bf16[256,2048]{1,0:T(8,128)(2,1)S(1)}, bf16[256,2048]{1,0:T(8,128)(2,1)S(1)}, u32[]{:S(2)}, u32[]{:S(2)}) collective-permute-start(bf16[256,2048]{1,0:T(8,128)(2,1)S(1)} %fusion.16), channel_id=1, source_target_pairs={{0,32},{16,48},{32,0},{48,16},{64,96},{80,112},{96,64},{112,80},{1... | collective-permute-start | bytes 3145736 | tf_op jit(solution)/shard_map/ppermute | solution.py:36
  18.5 23.9 %collective-permute-start.3 = (bf16[256,2048]{1,0:T(8,128)(2,1)S(1)}, bf16[256,2048]{1,0:T(8,128)(2,1)S(1)}, u32[]{:S(2)}, u32[]{:S(2)}) collective-permute-start(bf16[256,2048]{1,0:T(8,128)(2,1)S(1)} %fusion.16), channel_id=1, source_target_pairs={{0,16},{16,0},{32,48},{48,32},{64,80},{80,64},{96,112},{112,96},{1... | collective-permute-start | bytes 3145736 | tf_op jit(solution)/shard_map/ppermute | solution.py:36
  42.4 2.8 collective-permute-start.5
  42.4 1.0 copy-start.4
  69.4 32.5 %copy-start.1 = (s32[256,4]{0,1:T(4,128)S(1)}, s32[256,4]{0,1:T(4,128)}, u32[]{:S(2)}) copy-start(s32[256,4]{0,1:T(4,128)} %param.12) | copy-start | bytes 12292
  71.7 15.0 %collective-permute-start.6 = (bf16[4,2,128,128]{3,2,1,0:T(8,128)(2,1)}, bf16[4,2,128,128]{3,2,1,0:T(8,128)(2,1)S(1)}, u32[]{:S(2)}, u32[]{:S(2)}) collective-permute-start(bf16[4,2,128,128]{3,2,1,0:T(8,128)(2,1)} %get-tuple-element.42), channel_id=1, source_target_pairs={{0,1},{1,2},{2,3},{3,0},{4,5},{5,6},{6,7},{7,4},{8,9},{9,10},{10,1... | collective-permute-start | bytes 786440 | tf_op jit(solution)/shard_map/ppermute | solution.py:45
  71.7 16.6 %collective-permute-start.7 = (bf16[4,2,128,128]{3,2,1,0:T(8,128)(2,1)}, bf16[4,2,128,128]{3,2,1,0:T(8,128)(2,1)}, u32[]{:S(2)}, u32[]{:S(2)}) collective-permute-start(bf16[4,2,128,128]{3,2,1,0:T(8,128)(2,1)} %get-tuple-element.42), channel_id=1, source_target_pairs={{0,2},{1,3},{2,0},{3,1},{4,6},{5,7},{6,4},{7,5},{8,10},{9,11},{10,... | collective-permute-start | bytes 786440 | tf_op jit(solution)/shard_map/ppermute | solution.py:45
  73.7 22.9 %collective-permute-start.8 = (bf16[4,2,128,128]{3,2,1,0:T(8,128)(2,1)}, bf16[4,2,128,128]{3,2,1,0:T(8,128)(2,1)}, u32[]{:S(2)}, u32[]{:S(2)}) collective-permute-start(bf16[4,2,128,128]{3,2,1,0:T(8,128)(2,1)} %get-tuple-element.42), channel_id=1, source_target_pairs={{0,3},{1,0},{2,1},{3,2},{4,7},{5,4},{6,5},{7,6},{8,11},{9,8},{10,9... | collective-permute-start | bytes 786440 | tf_op jit(solution)/shard_map/ppermute | solution.py:45
  75.6 26.3 %collective-permute-start = (f32[2,128,128]{2,1,0:T(8,128)S(1)}, f32[2,128,128]{2,1,0:T(8,128)}, u32[]{:S(2)}, u32[]{:S(2)}) collective-permute-start(f32[2,128,128]{2,1,0:T(8,128)S(1)} %get-tuple-element.37), channel_id=1, source_target_pairs={{0,16},{16,0},{32,48},{48,32},{64,80},{80,64},{96,112},{112,96},{1... | collective-permute-start | bytes 393224 | tf_op jit(solution)/shard_map/ppermute | solution.py:36
  98.4 10.3 %collective-permute-start.10 = (bf16[4,2,128,128]{3,2,1,0:T(8,128)(2,1)}, bf16[4,2,128,128]{3,2,1,0:T(8,128)(2,1)}, u32[]{:S(2)}, u32[]{:S(2)}) collective-permute-start(bf16[4,2,128,128]{3,2,1,0:T(8,128)(2,1)} %fusion.40), channel_id=1, source_target_pairs={{0,8},{1,9},{2,10},{3,11},{4,12},{5,13},{6,14},{7,15},{8,0},{9,1},... | collective-permute-start | bytes 786440 | tf_op jit(solution)/shard_map/ppermute | solution.py:45
  99.4 9.8 %collective-permute-start.11 = (bf16[4,2,128,128]{3,2,1,0:T(8,128)(2,1)}, bf16[4,2,128,128]{3,2,1,0:T(8,128)(2,1)}, u32[]{:S(2)}, u32[]{:S(2)}) collective-permute-start(bf16[4,2,128,128]{3,2,1,0:T(8,128)(2,1)} %fusion.40), channel_id=1, source_target_pairs={{0,12},{1,13},{2,14},{3,15},{4,0},{5,1},{6,2},{7,3},{8,4},{9,5},{1... | collective-permute-start | bytes 786440 | tf_op jit(solution)/shard_map/ppermute | solution.py:45
  99.4 11.9 %collective-permute-start.9 = (bf16[4,2,128,128]{3,2,1,0:T(8,128)(2,1)}, bf16[4,2,128,128]{3,2,1,0:T(8,128)(2,1)}, u32[]{:S(2)}, u32[]{:S(2)}) collective-permute-start(bf16[4,2,128,128]{3,2,1,0:T(8,128)(2,1)} %fusion.40), channel_id=1, source_target_pairs={{0,4},{1,5},{2,6},{3,7},{4,8},{5,9},{6,10},{7,11},{8,12},{9,13},{1... | collective-permute-start | bytes 786440 | tf_op jit(solution)/shard_map/ppermute | solution.py:45
  101.5 6.5 %collective-permute-start.1 = (f32[2,128,128]{2,1,0:T(8,128)}, f32[2,128,128]{2,1,0:T(8,128)}, u32[]{:S(2)}, u32[]{:S(2)}) collective-permute-start(f32[2,128,128]{2,1,0:T(8,128)} %get-tuple-element.39), channel_id=1, source_target_pairs={{0,32},{16,48},{32,0},{48,16},{64,96},{80,112},{96,64},{112,80},{1... | collective-permute-start | bytes 393224 | tf_op jit(solution)/shard_map/ppermute | solution.py:36
  101.9 6.1 %collective-permute-start.2 = (f32[2,128,128]{2,1,0:T(8,128)}, f32[2,128,128]{2,1,0:T(8,128)}, u32[]{:S(2)}, u32[]{:S(2)}) collective-permute-start(f32[2,128,128]{2,1,0:T(8,128)} %get-tuple-element.38), channel_id=1, source_target_pairs={{0,48},{16,32},{32,16},{48,0},{64,112},{80,96},{96,80},{112,64},{1... | collective-permute-start | bytes 393224 | tf_op jit(solution)/shard_map/ppermute | solution.py:36
  119.1 6.4 %collective-permute-start.13 = (bf16[256,256]{0,1:T(8,128)(2,1)S(1)}, bf16[256,256]{0,1:T(8,128)(2,1)S(1)}, u32[]{:S(2)}, u32[]{:S(2)}) collective-permute-start(bf16[256,256]{0,1:T(8,128)(2,1)S(1)} %bitcast.125), channel_id=1, source_target_pairs={{0,32},{16,48},{32,0},{48,16},{64,96},{80,112},{96,64},{112,80},{1... | collective-permute-start | bytes 393224 | tf_op jit(solution)/shard_map/ppermute | solution.py:36
  119.7 5.8 %collective-permute-start.14 = (bf16[256,256]{0,1:T(8,128)(2,1)S(1)}, bf16[256,256]{0,1:T(8,128)(2,1)S(1)}, u32[]{:S(2)}, u32[]{:S(2)}) collective-permute-start(bf16[256,256]{0,1:T(8,128)(2,1)S(1)} %bitcast.123), channel_id=1, source_target_pairs={{0,48},{16,32},{32,16},{48,0},{64,112},{80,96},{96,80},{112,64},{1... | collective-permute-start | bytes 393224 | tf_op jit(solution)/shard_map/ppermute | solution.py:36
  119.7 5.8 %collective-permute-start.12 = (bf16[256,256]{0,1:T(8,128)(2,1)S(1)}, bf16[256,256]{0,1:T(8,128)(2,1)S(1)}, u32[]{:S(2)}, u32[]{:S(2)}) collective-permute-start(bf16[256,256]{0,1:T(8,128)(2,1)S(1)} %bitcast.121), channel_id=1, source_target_pairs={{0,16},{16,0},{32,48},{48,32},{64,80},{80,64},{96,112},{112,96},{1... | collective-permute-start | bytes 393224 | tf_op jit(solution)/shard_map/ppermute | solution.py:36
  133.1 11.9 %collective-permute-start.15 = (bf16[1,96,2048]{2,1,0:T(8,128)(2,1)S(1)}, bf16[1,96,2048]{2,1,0:T(8,128)(2,1)S(1)}, u32[]{:S(2)}, u32[]{:S(2)}) collective-permute-start(bf16[1,96,2048]{2,1,0:T(8,128)(2,1)S(1)} %get-tuple-element.21), channel_id=1, source_target_pairs={{0,1},{1,0},{2,3},{3,2},{4,5},{5,4},{6,7},{7,6},{8,9},{9,8},{10,11... | collective-permute-start | bytes 1179656 | tf_op jit(solution)/shard_map/ppermute | solution.py:146
  135.5 37.4 %collective-permute-start.16 = (bf16[1,96,2048]{2,1,0:T(8,128)(2,1)S(1)}, bf16[1,96,2048]{2,1,0:T(8,128)(2,1)S(1)}, u32[]{:S(2)}, u32[]{:S(2)}) collective-permute-start(bf16[1,96,2048]{2,1,0:T(8,128)(2,1)S(1)} %get-tuple-element.20), channel_id=1, source_target_pairs={{0,2},{1,3},{2,0},{3,1},{4,6},{5,7},{6,4},{7,5},{8,10},{9,11},{10,... | collective-permute-start | bytes 1179656 | tf_op jit(solution)/shard_map/ppermute | solution.py:146
  138.0 36.4 %collective-permute-start.17 = (bf16[1,96,2048]{2,1,0:T(8,128)(2,1)S(1)}, bf16[1,96,2048]{2,1,0:T(8,128)(2,1)S(1)}, u32[]{:S(2)}, u32[]{:S(2)}) collective-permute-start(bf16[1,96,2048]{2,1,0:T(8,128)(2,1)S(1)} %get-tuple-element.19), channel_id=1, source_target_pairs={{0,3},{1,2},{2,1},{3,0},{4,7},{5,6},{6,5},{7,4},{8,11},{9,10},{10,... | collective-permute-start | bytes 1179656 | tf_op jit(solution)/shard_map/ppermute | solution.py:146
  138.3 37.8 %collective-permute-start.18 = (bf16[1,96,2048]{2,1,0:T(8,128)(2,1)S(1)}, bf16[1,96,2048]{2,1,0:T(8,128)(2,1)S(1)}, u32[]{:S(2)}, u32[]{:S(2)}) collective-permute-start(bf16[1,96,2048]{2,1,0:T(8,128)(2,1)S(1)} %get-tuple-element.18), channel_id=1, source_target_pairs={{0,4},{1,5},{2,6},{3,7},{4,0},{5,1},{6,2},{7,3},{8,12},{9,13},{10,... | collective-permute-start | bytes 1179656 | tf_op jit(solution)/shard_map/ppermute | solution.py:146
  139.5 39.9 %collective-permute-start.19 = (bf16[1,96,2048]{2,1,0:T(8,128)(2,1)S(1)}, bf16[1,96,2048]{2,1,0:T(8,128)(2,1)S(1)}, u32[]{:S(2)}, u32[]{:S(2)}) collective-permute-start(bf16[1,96,2048]{2,1,0:T(8,128)(2,1)S(1)} %get-tuple-element.17), channel_id=1, source_target_pairs={{0,5},{1,4},{2,7},{3,6},{4,1},{5,0},{6,3},{7,2},{8,13},{9,12},{10,... | collective-permute-start | bytes 1179656 | tf_op jit(solution)/shard_map/ppermute | solution.py:146
  145.0 39.7 %collective-permute-start.20 = (bf16[1,96,2048]{2,1,0:T(8,128)(2,1)S(1)}, bf16[1,96,2048]{2,1,0:T(8,128)(2,1)S(1)}, u32[]{:S(2)}, u32[]{:S(2)}) collective-permute-start(bf16[1,96,2048]{2,1,0:T(8,128)(2,1)S(1)} %get-tuple-element.16), channel_id=1, source_target_pairs={{0,6},{1,7},{2,4},{3,5},{4,2},{5,3},{6,0},{7,1},{8,14},{9,15},{10,... | collective-permute-start | bytes 1179656 | tf_op jit(solution)/shard_map/ppermute | solution.py:146
  173.0 14.6 %collective-permute-start.21 = (bf16[1,96,2048]{2,1,0:T(8,128)(2,1)S(1)}, bf16[1,96,2048]{2,1,0:T(8,128)(2,1)S(1)}, u32[]{:S(2)}, u32[]{:S(2)}) collective-permute-start(bf16[1,96,2048]{2,1,0:T(8,128)(2,1)S(1)} %get-tuple-element.15), channel_id=1, source_target_pairs={{0,7},{1,6},{2,5},{3,4},{4,3},{5,2},{6,1},{7,0},{8,15},{9,14},{10,... | collective-permute-start | bytes 1179656 | tf_op jit(solution)/shard_map/ppermute | solution.py:146
  174.4 18.6 %collective-permute-start.22 = (bf16[1,96,2048]{2,1,0:T(8,128)(2,1)S(1)}, bf16[1,96,2048]{2,1,0:T(8,128)(2,1)S(1)}, u32[]{:S(2)}, u32[]{:S(2)}) collective-permute-start(bf16[1,96,2048]{2,1,0:T(8,128)(2,1)S(1)} %get-tuple-element.14), channel_id=1, source_target_pairs={{0,8},{1,9},{2,10},{3,11},{4,12},{5,13},{6,14},{7,15},{8,0},{9,1},... | collective-permute-start | bytes 1179656 | tf_op jit(solution)/shard_map/ppermute | solution.py:146
  176.1 25.8 %collective-permute-start.23 = (bf16[1,96,2048]{2,1,0:T(8,128)(2,1)S(1)}, bf16[1,96,2048]{2,1,0:T(8,128)(2,1)S(1)}, u32[]{:S(2)}, u32[]{:S(2)}) collective-permute-start(bf16[1,96,2048]{2,1,0:T(8,128)(2,1)S(1)} %get-tuple-element.13), channel_id=1, source_target_pairs={{0,9},{1,8},{2,11},{3,10},{4,13},{5,12},{6,15},{7,14},{8,1},{9,0},... | collective-permute-start | bytes 1179656 | tf_op jit(solution)/shard_map/ppermute | solution.py:146
  179.4 31.0 %collective-permute-start.24 = (bf16[1,96,2048]{2,1,0:T(8,128)(2,1)S(1)}, bf16[1,96,2048]{2,1,0:T(8,128)(2,1)S(1)}, u32[]{:S(2)}, u32[]{:S(2)}) collective-permute-start(bf16[1,96,2048]{2,1,0:T(8,128)(2,1)S(1)} %get-tuple-element.12), channel_id=1, source_target_pairs={{0,10},{1,11},{2,8},{3,9},{4,14},{5,15},{6,12},{7,13},{8,2},{9,3},... | collective-permute-start | bytes 1179656 | tf_op jit(solution)/shard_map/ppermute | solution.py:146
  184.7 35.5 %collective-permute-start.25 = (bf16[1,96,2048]{2,1,0:T(8,128)(2,1)S(1)}, bf16[1,96,2048]{2,1,0:T(8,128)(2,1)S(1)}, u32[]{:S(2)}, u32[]{:S(2)}) collective-permute-start(bf16[1,96,2048]{2,1,0:T(8,128)(2,1)S(1)} %get-tuple-element.11), channel_id=1, source_target_pairs={{0,11},{1,10},{2,9},{3,8},{4,15},{5,14},{6,13},{7,12},{8,3},{9,2},... | collective-permute-start | bytes 1179656 | tf_op jit(solution)/shard_map/ppermute | solution.py:146
  187.6 38.5 %collective-permute-start.26 = (bf16[1,96,2048]{2,1,0:T(8,128)(2,1)S(1)}, bf16[1,96,2048]{2,1,0:T(8,128)(2,1)S(1)}, u32[]{:S(2)}, u32[]{:S(2)}) collective-permute-start(bf16[1,96,2048]{2,1,0:T(8,128)(2,1)S(1)} %get-tuple-element.10), channel_id=1, source_target_pairs={{0,12},{1,13},{2,14},{3,15},{4,8},{5,9},{6,10},{7,11},{8,4},{9,5},... | collective-permute-start | bytes 1179656 | tf_op jit(solution)/shard_map/ppermute | solution.py:146
  193.0 41.8 %collective-permute-start.27 = (bf16[1,96,2048]{2,1,0:T(8,128)(2,1)S(1)}, bf16[1,96,2048]{2,1,0:T(8,128)(2,1)S(1)}, u32[]{:S(2)}, u32[]{:S(2)}) collective-permute-start(bf16[1,96,2048]{2,1,0:T(8,128)(2,1)S(1)} %get-tuple-element.9), channel_id=1, source_target_pairs={{0,13},{1,12},{2,15},{3,14},{4,9},{5,8},{6,11},{7,10},{8,5},{9,4},... | collective-permute-start | bytes 1179656 | tf_op jit(solution)/shard_map/ppermute | solution.py:146
  201.9 41.6 %collective-permute-start.28 = (bf16[1,96,2048]{2,1,0:T(8,128)(2,1)S(1)}, bf16[1,96,2048]{2,1,0:T(8,128)(2,1)S(1)}, u32[]{:S(2)}, u32[]{:S(2)}) collective-permute-start(bf16[1,96,2048]{2,1,0:T(8,128)(2,1)S(1)} %get-tuple-element.8), channel_id=1, source_target_pairs={{0,14},{1,15},{2,12},{3,13},{4,10},{5,11},{6,8},{7,9},{8,6},{9,7},... | collective-permute-start | bytes 1179656 | tf_op jit(solution)/shard_map/ppermute | solution.py:146
  210.5 43.8 %collective-permute-start.29 = (bf16[1,96,2048]{2,1,0:T(8,128)(2,1)S(1)}, bf16[1,96,2048]{2,1,0:T(8,128)(2,1)S(1)}, u32[]{:S(2)}, u32[]{:S(2)}) collective-permute-start(bf16[1,96,2048]{2,1,0:T(8,128)(2,1)S(1)} %get-tuple-element.7), channel_id=1, source_target_pairs={{0,15},{1,14},{2,13},{3,12},{4,11},{5,10},{6,9},{7,8},{8,7},{9,6},... | collective-permute-start | bytes 1179656 | tf_op jit(solution)/shard_map/ppermute | solution.py:146
  261.4 17.6 %copy-start.3 = (bf16[1,1024,2048]{2,1,0:T(8,128)(2,1)S(1)}, bf16[1,1024,2048]{2,1,0:T(8,128)(2,1)}, u32[]{:S(2)}) copy-start(bf16[1,1024,2048]{2,1,0:T(8,128)(2,1)} %param.15) | copy-start | bytes 12582916
  287.7 7.1 %copy-start.2 = (f32[256,4]{0,1:T(4,128)S(1)}, f32[256,4]{0,1:T(4,128)}, u32[]{:S(2)}) copy-start(f32[256,4]{0,1:T(4,128)} %param.13) | copy-start | bytes 12292
  287.7 116.1 %all-to-all-start.1 = ((bf16[16,96,2048]{2,1,0:T(8,128)(2,1)}), bf16[16,96,2048]{2,1,0:T(8,128)(2,1)}, u32[]{:S(2)}, u32[]{:S(2)}) async-start(bf16[16,96,2048]{2,1,0:T(8,128)(2,1)} %bitcast.118), calls=%async_computation.1 | async-start | bytes 12582912 | tf_op jit(solution)/shard_map/all_to_all | solution.py:154
Sparse Core Ops, SparseCore 0:
  9.5 89.8 all-gather.1
